TPU v7x, 32 devices: a whole 2x2x4 slice. The times are simulated.
32 devices in a mesh: sec: 4 (over z), blk: 8 (over y, x, core).
Axes of the slice: x: 2, y: 2, z: 4, core: 2. Of those that a mesh axis runs over, the one named last changes fastest.
Arguments:
- raw: bfloat16 [32, 128, 256], P(('sec', 'blk')), may hold values from -6 to 6
- tissue: int32 [4, 8, 4], P('sec', 'blk'), may hold values 0 or 1
- w_emb: bfloat16 [32, 3, 3], replicated, may hold values from -3 to 3
- w_one: bfloat16 [32, 32, 3, 3], replicated, may hold values from -0.5 to 0.5
- w_down: bfloat16 [64, 32, 2, 2], replicated, may hold values from -0.75 to 0.75
- w_deep: bfloat16 [64, 64, 3, 3, 3], replicated, may hold values from -0.21875 to 0.21875
- w_up: bfloat16 [32, 64, 2, 2], replicated, may hold values from -1 to 1
- w_out: bfloat16 [3, 32], replicated, may hold values from -1 to 1
Outputs:
- logits: float32 [3, 32, 128, 256], P(None, 'sec', 'blk')
Inputs may be any that keep to these rules, and one draw needn't show every extreme that they name: 1 marks a block of 8 sections, 16 columns and one 4-th of the rows that holds tissue, 0 one without.
All inputs are finite; a program needn't handle non-finite values.
Results may differ from a plain program's by a relative error of at most 0.0067.
Values may be sent and summed in bfloat16 or wider, within the bound.
A program may use at most 256 MiB of HBM per device.

v0:
```python
import jax
import jax.numpy as jnp
from jax import lax
from jax.sharding import PartitionSpec as P


def extended(value, sides, width):
    for axis, dim in sides:
        peers, length = (lax.axis_size(axis), value.shape[dim])
        up = [(i, (i + 1) % peers) for i in range(peers - 1)]
        down = [(j, i) for i, j in up]
        last = lax.slice_in_dim(value, length - width, length, axis=dim)
        leading = lax.slice_in_dim(value, 0, width, axis=dim)
        before = lax.ppermute(last, axis, up)
        after = lax.ppermute(leading, axis, down)
        value = jnp.concatenate([before, value, after], axis=dim)
    return value


def embed(padded, w_emb, columns_out, length_y):
    stacked = []
    for offset_x in range(3):
        for offset_y in range(3):
            stacked.append(
                padded[:, offset_x : offset_x + columns_out, offset_y : offset_y + length_y]
            )
    stacked = jnp.stack(stacked, 0)
    weights = w_emb.reshape(w_emb.shape[0], 9)
    summed = jnp.einsum("ck,kzxy->czxy", weights, stacked, preferred_element_type=jnp.float32)
    return jnp.maximum(summed, 0.0).astype(jnp.bfloat16)


def conv_plane(padded, weights, width_x, length_y):
    summed = None
    for offset_x in range(3):
        for offset_y in range(3):
            window = padded[:, :, offset_x : offset_x + width_x, offset_y : offset_y + length_y]
            contribution = jnp.einsum(
                "oc,czxy->ozxy",
                weights[:, :, offset_x, offset_y],
                window,
                preferred_element_type=jnp.float32,
            )
            summed = contribution if summed is None else summed + contribution
    return summed


def conv_volume(padded, weights, depth_z, width_x, length_y):
    summed = None
    for offset_z in range(3):
        for offset_x in range(3):
            for offset_y in range(3):
                window = padded[
                    :,
                    offset_z : offset_z + depth_z,
                    offset_x : offset_x + width_x,
                    offset_y : offset_y + length_y,
                ]
                contribution = jnp.einsum(
                    "oc,czxy->ozxy",
                    weights[:, :, offset_z, offset_x, offset_y],
                    window,
                    preferred_element_type=jnp.float32,
                )
                summed = contribution if summed is None else summed + contribution
    return summed


def per_device(raw, tissue, w_emb, w_one, w_down, w_deep, w_up, w_out):
    sections = lax.all_to_all(raw, "blk", split_axis=1, concat_axis=0, tiled=True)
    depth_z, width_x, length_y = sections.shape
    blocks_y = tissue.shape[2]
    span_y = length_y // blocks_y
    half_x = width_x // 2
    half_y = length_y // 2
    half_span = span_y // 2
    channels = w_emb.shape[0]
    flags = tissue[0, 0].astype(jnp.float32)
    mask_full = jnp.repeat(flags, span_y)
    mask_half = jnp.repeat(flags, half_span)
    masked = sections * mask_full.astype(jnp.bfloat16)
    narrow = extended(masked, (("blk", 1),), 1)
    narrow = jnp.pad(narrow, ((0, 0), (0, 0), (1, 1)))
    local_emb = embed(narrow, w_emb, width_x, length_y)
    embedded = extended(local_emb, (("blk", 2),), 1)
    embedded = jnp.pad(embedded, ((0, 0), (0, 0), (0, 0), (1, 1)))
    first_sum = conv_plane(embedded, w_one, width_x, length_y)
    features = (jnp.maximum(first_sum, 0.0) * mask_full).astype(jnp.bfloat16)
    shaped = features.reshape(channels, depth_z, half_x, 2, half_y, 2)
    lowered = jnp.einsum("ocab,czxayb->ozxy", w_down, shaped, preferred_element_type=jnp.float32)
    down = (jnp.maximum(lowered, 0.0) * mask_half).astype(jnp.bfloat16)
    rimmed = extended(down, (("sec", 1), ("blk", 2)), 1)
    rimmed = jnp.pad(rimmed, ((0, 0), (0, 0), (0, 0), (1, 1)))
    deep_sum = conv_volume(rimmed, w_deep, depth_z, half_x, half_y)
    deep = (jnp.maximum(deep_sum, 0.0) * mask_half).astype(jnp.bfloat16)
    raised = jnp.einsum("ocab,czxy->ozxayb", w_up, deep, preferred_element_type=jnp.float32)
    raised = raised.reshape(channels, depth_z, width_x, length_y)
    decoded = (jnp.maximum(raised + features.astype(jnp.float32), 0.0) * mask_full).astype(
        jnp.bfloat16
    )
    logits = jnp.einsum("oc,czxy->ozxy", w_out, decoded, preferred_element_type=jnp.float32)
    return logits * mask_full


def solution(mesh):
    placed = (P(("sec", "blk"), None, None), P("sec", "blk", None), P(), P(), P(), P(), P(), P())
    return jax.shard_map(
        per_device,
        mesh=mesh,
        in_specs=placed,
        out_specs=P(None, "sec", "blk", None),
        check_vma=False,
    )
```

profile of v0, /device:TPU:11, one launch (start us, length us, event | category | flops | bytes accessed | tf_op | source)
XLA Modules:
  0.0 189.1 jit_solution(16628197516298694183)
XLA Ops:
  3.1 4.6 %all-to-all-start = ((bf16[8,2,2048]{2,1,0:T(2,128)(2,1)}), bf16[8,2,2048]{2,1,0:T(2,128)(2,1)S(1)}, u32[]{:S(2)}, u32[]{:S(2)}) async-start(bf16[8,2,2048]{2,1,0:T(2,128)(2,1)} %reshape.77), calls=%async_computation | async-start | bytes 131072 | tf_op jit(solution)/shard_map/all_to_all | solution.py:70
  11.2 3.5 %collective-permute-start = (bf16[8,1,256]{2,1,0:T(2,128)(2,1)S(1)}, bf16[8,1,256]{2,1,0:T(2,128)(2,1)S(1)}, u32[]{:S(2)}, u32[]{:S(2)}) collective-permute-start(bf16[8,1,256]{2,1,0:T(2,128)(2,1)S(1)} %get-tuple-element.21), channel_id=1, source_target_pairs={{0,1},{1,2},{2,3},{3,4},{4,5},{5,6},{6,7},{8,9},{9,10},{10,11},{11... | collective-permute-start | bytes 12296 | tf_op jit(solution)/shard_map/ppermute | solution.py:14
  14.7 1.9 %collective-permute-start.1 = (bf16[8,1,256]{2,1,0:T(2,128)(2,1)S(1)}, bf16[8,1,256]{2,1,0:T(2,128)(2,1)S(1)}, u32[]{:S(2)}, u32[]{:S(2)}) collective-permute-start(bf16[8,1,256]{2,1,0:T(2,128)(2,1)S(1)} %get-tuple-element.22), channel_id=1, source_target_pairs={{1,0},{2,1},{3,2},{4,3},{5,4},{6,5},{7,6},{9,8},{10,9},{11,10},{12... | collective-permute-start | bytes 12296 | tf_op jit(solution)/shard_map/ppermute | solution.py:15
  16.8 3.8 %collective-permute-done.1 = bf16[8,1,256]{2,1,0:T(2,128)(2,1)S(1)} collective-permute-done((bf16[8,1,256]{2,1,0:T(2,128)(2,1)S(1)}, bf16[8,1,256]{2,1,0:T(2,128)(2,1)S(1)}, u32[]{:S(2)}, u32[]{:S(2)}) %collective-permute-start.1) | collective-permute-done | bytes 4128 | tf_op jit(solution)/shard_map/ppermute | solution.py:15
  24.5 1.9 %collective-permute-start.2 = (bf16[32,8,1,256]{3,0,2,1:T(8,128)(2,1)S(1)}, bf16[32,8,1,256]{3,0,2,1:T(8,128)(2,1)S(1)}, u32[]{:S(2)}, u32[]{:S(2)}) collective-permute-start(bf16[32,8,1,256]{3,0,2,1:T(8,128)(2,1)S(1)} %get-tuple-element.5), channel_id=1, source_target_pairs={{0,1},{1,2},{2,3},{3,4},{4,5},{5,6},{6,7},{8,9},{9,10},{10,11},{11... | collective-permute-start | bytes 393224 | tf_op jit(solution)/shard_map/ppermute | solution.py:14
  26.5 2.6 %collective-permute-start.3 = (bf16[32,8,1,256]{3,0,2,1:T(8,128)(2,1)S(1)}, bf16[32,8,1,256]{3,0,2,1:T(8,128)(2,1)S(1)}, u32[]{:S(2)}, u32[]{:S(2)}) collective-permute-start(bf16[32,8,1,256]{3,0,2,1:T(8,128)(2,1)S(1)} %get-tuple-element.6), channel_id=1, source_target_pairs={{1,0},{2,1},{3,2},{4,3},{5,4},{6,5},{7,6},{9,8},{10,9},{11,10},{12... | collective-permute-start | bytes 393224 | tf_op jit(solution)/shard_map/ppermute | solution.py:15
  29.1 2.6 %fusion.175 = f32[8,16,256,32]{2,3,1,0:T(8,128)} fusion(bf16[32,8,16,256]{3,0,2,1:T(8,128)(2,1)S(1)} %fusion.41, bf16[32,32,3,3]{1,0,3,2:T(8,128)(2,1)S(1)} %copy-done.4), kind=kOutput, calls=%fused_computation.206 | convolution fusion | flops 67108864 | bytes 6299648 | tf_op jit(solution)/shard_map/oc,czxy->ozxy/dot_general | solution.py:38
  31.7 2.0 %collective-permute-done.3 = bf16[32,8,1,256]{3,0,2,1:T(8,128)(2,1)S(1)} collective-permute-done((bf16[32,8,1,256]{3,0,2,1:T(8,128)(2,1)S(1)}, bf16[32,8,1,256]{3,0,2,1:T(8,128)(2,1)S(1)}, u32[]{:S(2)}, u32[]{:S(2)}) %collective-permute-start.3) | collective-permute-done | bytes 131104 | tf_op jit(solution)/shard_map/ppermute | solution.py:15
  33.7 2.4 %fusion.8 = bf16[32,8,18,258]{3,0,2,1:T(8,128)(2,1)S(1)} fusion(bf16[32,8,1,256]{3,0,2,1:T(8,128)(2,1)S(1)} %collective-permute-done.3, bf16[32,8,16,256]{3,0,2,1:T(8,128)(2,1)S(1)} %fusion.41, bf16[32,8,1,256]{3,0,2,1:T(8,128)(2,1)S(1)} %collective-permute-done.2), kind=kLoop, calls=%fused_computation.15 | loop fusion | flops 14266368 | bytes 4737024 | tf_op jit(solution)/shard_map/concatenate | solution.py:16
  36.1 2.7 %fusion.20 = f32[8,16,256,32]{2,3,1,0:T(8,128)} fusion(bf16[32,8,18,258]{3,0,2,1:T(8,128)(2,1)S(1)} %fusion.8, bf16[32,32,3,3]{1,0,3,2:T(8,128)(2,1)S(1)} %copy-done.4), kind=kOutput, calls=%fused_computation.29 | convolution fusion | flops 67108864 | bytes 6299648 | tf_op jit(solution)/shard_map/oc,czxy->ozxy/dot_general | solution.py:38
  38.7 2.8 %fusion.22 = f32[8,16,256,32]{2,3,1,0:T(8,128)} fusion(bf16[32,8,18,258]{3,0,2,1:T(8,128)(2,1)S(1)} %fusion.8, bf16[32,32,3,3]{1,0,3,2:T(8,128)(2,1)S(1)} %copy-done.4), kind=kOutput, calls=%fused_computation.31 | convolution fusion | flops 67108864 | bytes 6299648 | tf_op jit(solution)/shard_map/oc,czxy->ozxy/dot_general | solution.py:38
  41.5 2.6 %fusion.24 = f32[8,16,256,32]{2,3,1,0:T(8,128)} fusion(bf16[32,8,18,258]{3,0,2,1:T(8,128)(2,1)S(1)} %fusion.8, bf16[32,32,3,3]{1,0,3,2:T(8,128)(2,1)S(1)} %copy-done.4), kind=kOutput, calls=%fused_computation.33 | convolution fusion | flops 67108864 | bytes 6299648 | tf_op jit(solution)/shard_map/oc,czxy->ozxy/dot_general | solution.py:38
  44.1 2.8 %fusion.26 = f32[8,16,256,32]{2,3,1,0:T(8,128)} fusion(bf16[32,8,18,258]{3,0,2,1:T(8,128)(2,1)S(1)} %fusion.8, bf16[32,32,3,3]{1,0,3,2:T(8,128)(2,1)S(1)} %copy-done.4), kind=kOutput, calls=%fused_computation.35 | convolution fusion | flops 67108864 | bytes 6299648 | tf_op jit(solution)/shard_map/oc,czxy->ozxy/dot_general | solution.py:38
  46.9 2.7 %fusion.30 = f32[8,16,256,32]{2,3,1,0:T(8,128)} fusion(bf16[32,8,18,258]{3,0,2,1:T(8,128)(2,1)S(1)} %fusion.8, bf16[32,32,3,3]{1,0,3,2:T(8,128)(2,1)S(1)} %copy-done.4), kind=kOutput, calls=%fused_computation.40 | convolution fusion | flops 67108864 | bytes 6299648 | tf_op jit(solution)/shard_map/oc,czxy->ozxy/dot_general | solution.py:38
  50.3 2.6 %fusion.18 = f32[8,16,256,32]{2,3,1,0:T(8,128)} fusion(bf16[32,8,1,256]{3,0,2,1:T(8,128)(2,1)S(1)} %collective-permute-done.3, bf16[32,8,16,256]{3,0,2,1:T(8,128)(2,1)S(1)} %fusion.41, bf16[32,32,3,3]{1,0,3,2:T(8,128)(2,1)S(1)} %copy-done.4), kind=kOutput, calls=%fused_computation.27 | convolution fusion | flops 71303168 | bytes 6430720 | tf_op jit(solution)/shard_map/oc,czxy->ozxy/dot_general | solution.py:38
  52.9 10.9 %fusion.38 = bf16[32,8,16,256]{3,0,2,1:T(8,128)(2,1)S(1)} fusion(f32[256]{0:T(256)S(1)} %reshape.30, bf16[32,8,18,258]{3,0,2,1:T(8,128)(2,1)S(1)} %fusion.8, f32[8,16,256,32]{2,3,1,0:T(8,128)} %fusion.18, f32[8,16,256,32]{2,3,1,0:T(8,128)} %fusion.20, f32[8,16,256,32]{2,3,1,0:T(8,128)} %fusion.22, f32[8,16,256,32]{2,3,1,0:T(8,128)} %fusion.175, ...), kind=kOutput, calls=%fused_computation.59 | convolution fusion | flops 78643200 | bytes 37757952 | tf_op jit(solution)/shard_map/oc,czxy->ozxy/dot_general | solution.py:38
  63.9 6.7 %copy.169 = bf16[32,8,16,256]{0,1,3,2:T(8,128)(2,1)} copy(bf16[32,8,16,256]{3,0,2,1:T(8,128)(2,1)S(1)} %fusion.38) | data formatting | bytes 4194304 | tf_op jit(solution)/shard_map/convert_element_type | solution.py:88
  70.5 6.3 %fusion.45 = bf16[64,8,8,128]{3,0,2,1:T(8,128)(2,1)S(1)} fusion(bf16[32,8,8,2,128,2]{0,1,5,4,3,2:T(8,128)(2,1)} %bitcast.394, f32[128]{0:T(128)S(1)} %mul.67, bf16[64,32,2,2,1,1]{0,3,2,1,5,4:T(2,128)(2,1)S(1)} %bitcast.399), kind=kOutput, calls=%fused_computation.64 | convolution fusion | flops 135790592 | bytes 3162624 | tf_op jit(solution)/shard_map/ocab,czxayb->ozxy/dot_general | solution.py:90
  76.8 3.2 %collective-permute-start.4 = (bf16[64,1,8,128]{3,0,2,1:T(8,128)(2,1)S(1)}, bf16[64,1,8,128]{3,0,2,1:T(8,128)(2,1)S(1)}, u32[]{:S(2)}, u32[]{:S(2)}) collective-permute-start(bf16[64,1,8,128]{3,0,2,1:T(8,128)(2,1)S(1)} %get-tuple-element.11), channel_id=1, source_target_pairs={{0,8},{8,16},{16,24},{1,9},{9,17},{17,25},{2,10},{10,18},{18,26},{... | collective-permute-start | bytes 393224 | tf_op jit(solution)/shard_map/ppermute | solution.py:14
  80.0 2.1 %collective-permute-start.5 = (bf16[64,1,8,128]{3,0,2,1:T(8,128)(2,1)S(1)}, bf16[64,1,8,128]{3,0,2,1:T(8,128)(2,1)S(1)}, u32[]{:S(2)}, u32[]{:S(2)}) collective-permute-start(bf16[64,1,8,128]{3,0,2,1:T(8,128)(2,1)S(1)} %get-tuple-element.12), channel_id=1, source_target_pairs={{8,0},{16,8},{24,16},{9,1},{17,9},{25,17},{10,2},{18,10},{26,18},{... | collective-permute-start | bytes 393224 | tf_op jit(solution)/shard_map/ppermute | solution.py:15
  83.9 2.1 %collective-permute-done.5 = bf16[64,1,8,128]{3,0,2,1:T(8,128)(2,1)S(1)} collective-permute-done((bf16[64,1,8,128]{3,0,2,1:T(8,128)(2,1)S(1)}, bf16[64,1,8,128]{3,0,2,1:T(8,128)(2,1)S(1)}, u32[]{:S(2)}, u32[]{:S(2)}) %collective-permute-start.5) | collective-permute-done | bytes 131104 | tf_op jit(solution)/shard_map/ppermute | solution.py:15
  86.0 3.4 %collective-permute-start.6 = (bf16[64,10,1,128]{3,0,2,1:T(8,128)(2,1)S(1)}, bf16[64,10,1,128]{3,0,2,1:T(8,128)(2,1)S(1)}, u32[]{:S(2)}, u32[]{:S(2)}) collective-permute-start(bf16[64,10,1,128]{3,0,2,1:T(8,128)(2,1)S(1)} %get-tuple-element.9), channel_id=1, source_target_pairs={{0,1},{1,2},{2,3},{3,4},{4,5},{5,6},{6,7},{8,9},{9,10},{10,11},{11... | collective-permute-start | bytes 491528 | tf_op jit(solution)/shard_map/ppermute | solution.py:14
  89.4 1.9 %collective-permute-start.7 = (bf16[64,10,1,128]{3,0,2,1:T(8,128)(2,1)S(1)}, bf16[64,10,1,128]{3,0,2,1:T(8,128)(2,1)S(1)}, u32[]{:S(2)}, u32[]{:S(2)}) collective-permute-start(bf16[64,10,1,128]{3,0,2,1:T(8,128)(2,1)S(1)} %get-tuple-element.10), channel_id=1, source_target_pairs={{1,0},{2,1},{3,2},{4,3},{5,4},{6,5},{7,6},{9,8},{10,9},{11,10},{12... | collective-permute-start | bytes 491528 | tf_op jit(solution)/shard_map/ppermute | solution.py:15
  94.8 2.1 %collective-permute-done.7 = bf16[64,10,1,128]{3,0,2,1:T(8,128)(2,1)S(1)} collective-permute-done((bf16[64,10,1,128]{3,0,2,1:T(8,128)(2,1)S(1)}, bf16[64,10,1,128]{3,0,2,1:T(8,128)(2,1)S(1)}, u32[]{:S(2)}, u32[]{:S(2)}) %collective-permute-start.7) | collective-permute-done | bytes 163872 | tf_op jit(solution)/shard_map/ppermute | solution.py:15
  96.9 3.1 %select_maximum_fusion = bf16[64,10,10,130]{3,0,2,1:T(8,128)(2,1)S(1)} fusion(bf16[64,10,1,128]{3,0,2,1:T(8,128)(2,1)S(1)} %collective-permute-done.7, bf16[64,10,1,128]{3,0,2,1:T(8,128)(2,1)S(1)} %collective-permute-done.6, bf16[64,1,8,128]{3,0,2,1:T(8,128)(2,1)S(1)} %collective-permute-done.5, bf16[64,8,8,128]{3,0,2,1:T(8,128)(2,1)S(1)} %fusion.45, ...), kind=kLoop, calls=%fused_computation.16 | loop fusion | flops 14976000 | bytes 3302400 | tf_op jit(solution)/shard_map/concatenate | solution.py:16
  109.0 1.9 %fusion.68 = f32[8,8,128,64]{2,3,1,0:T(8,128)} fusion(bf16[64,10,10,130]{3,0,2,1:T(8,128)(2,1)S(1)} %select_maximum_fusion, bf16[64,64,3,3,3]{1,0,4,3,2:T(8,128)(2,1)S(1)} %copy-done.3), kind=kOutput, calls=%fused_computation.85 | convolution fusion | flops 67108864 | bytes 3162112 | tf_op jit(solution)/shard_map/oc,czxy->ozxy/dot_general | solution.py:59
  116.3 1.9 %fusion.78 = f32[8,8,128,64]{2,3,1,0:T(8,128)} fusion(bf16[64,10,10,130]{3,0,2,1:T(8,128)(2,1)S(1)} %select_maximum_fusion, bf16[64,64,3,3,3]{1,0,4,3,2:T(8,128)(2,1)S(1)} %copy-done.3), kind=kOutput, calls=%fused_computation.95 | convolution fusion | flops 67108864 | bytes 3162112 | tf_op jit(solution)/shard_map/oc,czxy->ozxy/dot_general | solution.py:59
  120.0 1.9 %fusion.84 = f32[8,8,128,64]{2,3,1,0:T(8,128)} fusion(bf16[64,10,10,130]{3,0,2,1:T(8,128)(2,1)S(1)} %select_maximum_fusion, bf16[64,64,3,3,3]{1,0,4,3,2:T(8,128)(2,1)S(1)} %copy-done.3), kind=kOutput, calls=%fused_computation.101 | convolution fusion | flops 67108864 | bytes 3162112 | tf_op jit(solution)/shard_map/oc,czxy->ozxy/dot_general | solution.py:59
  141.9 20.8 %convolution_bitcast_fusion = f32[32,8,8,2,128,2]{4,0,5,3,2,1:T(8,128)} fusion(f32[8,8,128,64]{2,3,1,0:T(8,128)} %fusion.52, f32[8,8,128,64]{2,3,1,0:T(8,128)} %fusion.54, f32[8,8,128,64]{2,3,1,0:T(8,128)} %fusion.56, f32[8,8,128,64]{2,3,1,0:T(8,128)} %fusion.58, f32[8,8,128,64]{2,3,1,0:T(8,128)} %fusion.60, f32[8,8,128,64]{2,3,1,0:T(8,128)} %fusion.62, ...), kind=kOutput, calls=%fused_computation.23 | convolution fusion | flops 216530944 | bytes 59818496 | tf_op jit(solution)/shard_map/ocab,czxy->ozxayb/dot_general | solution.py:96
  162.8 11.0 %copy.173 = f32[32,8,8,2,128,2]{0,1,5,4,3,2:T(8,128)} copy(f32[32,8,8,2,128,2]{4,0,5,3,2,1:T(8,128)} %convolution_bitcast_fusion) | data formatting | bytes 8388608 | tf_op jit(solution)/shard_map/ocab,czxy->ozxayb/transpose | solution.py:96
  173.7 11.5 %copy.174 = f32[32,8,16,256]{3,0,2,1:T(8,128)} copy(f32[32,8,16,256]{0,1,3,2:T(8,128)} %bitcast.393) | data formatting | bytes 8388608 | tf_op jit(solution)/shard_map/reshape | solution.py:97
  185.3 2.9 %fusion.49 = f32[3,8,16,256]{3,0,2,1:T(4,128)S(1)} fusion(f32[32,8,16,256]{3,0,2,1:T(8,128)} %copy.174, bf16[32,8,16,256]{3,0,2,1:T(8,128)(2,1)S(1)} %copy-done.2, f32[256]{0:T(256)S(1)} %reshape.30, bf16[3,32]{1,0:T(4,128)(2,1)S(1)} %copy-done.5), kind=kOutput, calls=%fused_computation.66 | convolution fusion | flops 11632640 | bytes 6685888 | tf_op jit(solution)/shard_map/oc,czxy->ozxy/dot_general | solution.py:101
  (77 shorter events, 53.5 us)
Async XLA Ops:
  0.0 141.9 %copy-start = (bf16[32,64,2,2]{1,3,2,0:T(2,128)(2,1)S(1)}, bf16[32,64,2,2]{1,3,2,0:T(2,128)(2,1)}, u32[]{:S(2)}) copy-start(bf16[32,64,2,2]{1,3,2,0:T(2,128)(2,1)} %param.14) | copy-start | bytes 49156
  3.1 7.9 %all-to-all-start = ((bf16[8,2,2048]{2,1,0:T(2,128)(2,1)}), bf16[8,2,2048]{2,1,0:T(2,128)(2,1)S(1)}, u32[]{:S(2)}, u32[]{:S(2)}) async-start(bf16[8,2,2048]{2,1,0:T(2,128)(2,1)} %reshape.77), calls=%async_computation | async-start | bytes 131072 | tf_op jit(solution)/shard_map/all_to_all | solution.py:70
  11.2 5.6 %collective-permute-start = (bf16[8,1,256]{2,1,0:T(2,128)(2,1)S(1)}, bf16[8,1,256]{2,1,0:T(2,128)(2,1)S(1)}, u32[]{:S(2)}, u32[]{:S(2)}) collective-permute-start(bf16[8,1,256]{2,1,0:T(2,128)(2,1)S(1)} %get-tuple-element.21), channel_id=1, source_target_pairs={{0,1},{1,2},{2,3},{3,4},{4,5},{5,6},{6,7},{8,9},{9,10},{10,11},{11... | collective-permute-start | bytes 12296 | tf_op jit(solution)/shard_map/ppermute | solution.py:14
  14.7 5.9 %collective-permute-start.1 = (bf16[8,1,256]{2,1,0:T(2,128)(2,1)S(1)}, bf16[8,1,256]{2,1,0:T(2,128)(2,1)S(1)}, u32[]{:S(2)}, u32[]{:S(2)}) collective-permute-start(bf16[8,1,256]{2,1,0:T(2,128)(2,1)S(1)} %get-tuple-element.22), channel_id=1, source_target_pairs={{1,0},{2,1},{3,2},{4,3},{5,4},{6,5},{7,6},{9,8},{10,9},{11,10},{12... | collective-permute-start | bytes 12296 | tf_op jit(solution)/shard_map/ppermute | solution.py:15
  23.7 5.3 %copy-start.4 = (bf16[32,32,3,3]{1,0,3,2:T(8,128)(2,1)S(1)}, bf16[32,32,3,3]{1,0,3,2:T(8,128)(2,1)}, u32[]{:S(2)}) copy-start(bf16[32,32,3,3]{1,0,3,2:T(8,128)(2,1)} %param.11) | copy-start | bytes 55300
  24.5 7.2 %collective-permute-start.2 = (bf16[32,8,1,256]{3,0,2,1:T(8,128)(2,1)S(1)}, bf16[32,8,1,256]{3,0,2,1:T(8,128)(2,1)S(1)}, u32[]{:S(2)}, u32[]{:S(2)}) collective-permute-start(bf16[32,8,1,256]{3,0,2,1:T(8,128)(2,1)S(1)} %get-tuple-element.5), channel_id=1, source_target_pairs={{0,1},{1,2},{2,3},{3,4},{4,5},{5,6},{6,7},{8,9},{9,10},{10,11},{11... | collective-permute-start | bytes 393224 | tf_op jit(solution)/shard_map/ppermute | solution.py:14
  26.5 7.2 %collective-permute-start.3 = (bf16[32,8,1,256]{3,0,2,1:T(8,128)(2,1)S(1)}, bf16[32,8,1,256]{3,0,2,1:T(8,128)(2,1)S(1)}, u32[]{:S(2)}, u32[]{:S(2)}) collective-permute-start(bf16[32,8,1,256]{3,0,2,1:T(8,128)(2,1)S(1)} %get-tuple-element.6), channel_id=1, source_target_pairs={{1,0},{2,1},{3,2},{4,3},{5,4},{6,5},{7,6},{9,8},{10,9},{11,10},{12... | collective-permute-start | bytes 393224 | tf_op jit(solution)/shard_map/ppermute | solution.py:15
  63.8 6.7 %copy-start.1 = (bf16[32,8,16,256]{3,0,2,1:T(8,128)(2,1)}, bf16[32,8,16,256]{3,0,2,1:T(8,128)(2,1)S(1)}, u32[]{:S(2)}) copy-start(bf16[32,8,16,256]{3,0,2,1:T(8,128)(2,1)S(1)} %fusion.38) | copy-start | bytes 6291460
  63.8 6.7 %copy-start.6 = (bf16[64,32,2,2]{0,3,2,1:T(2,128)(2,1)S(1)}, bf16[64,32,2,2]{0,3,2,1:T(2,128)(2,1)}, u32[]{:S(2)}) copy-start(bf16[64,32,2,2]{0,3,2,1:T(2,128)(2,1)} %param.12) | copy-start | bytes 49156
  70.5 11.6 %copy-start.3 = (bf16[64,64,3,3,3]{1,0,4,3,2:T(8,128)(2,1)S(1)}, bf16[64,64,3,3,3]{1,0,4,3,2:T(8,128)(2,1)}, u32[]{:S(2)}) copy-start(bf16[64,64,3,3,3]{1,0,4,3,2:T(8,128)(2,1)} %param.13) | copy-start | bytes 663556
  76.8 7.0 %collective-permute-start.4 = (bf16[64,1,8,128]{3,0,2,1:T(8,128)(2,1)S(1)}, bf16[64,1,8,128]{3,0,2,1:T(8,128)(2,1)S(1)}, u32[]{:S(2)}, u32[]{:S(2)}) collective-permute-start(bf16[64,1,8,128]{3,0,2,1:T(8,128)(2,1)S(1)} %get-tuple-element.11), channel_id=1, source_target_pairs={{0,8},{8,16},{16,24},{1,9},{9,17},{17,25},{2,10},{10,18},{18,26},{... | collective-permute-start | bytes 393224 | tf_op jit(solution)/shard_map/ppermute | solution.py:14
  80.0 5.9 %collective-permute-start.5 = (bf16[64,1,8,128]{3,0,2,1:T(8,128)(2,1)S(1)}, bf16[64,1,8,128]{3,0,2,1:T(8,128)(2,1)S(1)}, u32[]{:S(2)}, u32[]{:S(2)}) collective-permute-start(bf16[64,1,8,128]{3,0,2,1:T(8,128)(2,1)S(1)} %get-tuple-element.12), channel_id=1, source_target_pairs={{8,0},{16,8},{24,16},{9,1},{17,9},{25,17},{10,2},{18,10},{26,18},{... | collective-permute-start | bytes 393224 | tf_op jit(solution)/shard_map/ppermute | solution.py:15
  86.0 8.8 %collective-permute-start.6 = (bf16[64,10,1,128]{3,0,2,1:T(8,128)(2,1)S(1)}, bf16[64,10,1,128]{3,0,2,1:T(8,128)(2,1)S(1)}, u32[]{:S(2)}, u32[]{:S(2)}) collective-permute-start(bf16[64,10,1,128]{3,0,2,1:T(8,128)(2,1)S(1)} %get-tuple-element.9), channel_id=1, source_target_pairs={{0,1},{1,2},{2,3},{3,4},{4,5},{5,6},{6,7},{8,9},{9,10},{10,11},{11... | collective-permute-start | bytes 491528 | tf_op jit(solution)/shard_map/ppermute | solution.py:14
  89.4 7.5 %collective-permute-start.7 = (bf16[64,10,1,128]{3,0,2,1:T(8,128)(2,1)S(1)}, bf16[64,10,1,128]{3,0,2,1:T(8,128)(2,1)S(1)}, u32[]{:S(2)}, u32[]{:S(2)}) collective-permute-start(bf16[64,10,1,128]{3,0,2,1:T(8,128)(2,1)S(1)} %get-tuple-element.10), channel_id=1, source_target_pairs={{1,0},{2,1},{3,2},{4,3},{5,4},{6,5},{7,6},{9,8},{10,9},{11,10},{12... | collective-permute-start | bytes 491528 | tf_op jit(solution)/shard_map/ppermute | solution.py:15
  173.7 11.5 %copy-start.2 = (bf16[32,8,16,256]{3,0,2,1:T(8,128)(2,1)S(1)}, bf16[32,8,16,256]{3,0,2,1:T(8,128)(2,1)}, u32[]{:S(2)}) copy-start(bf16[32,8,16,256]{3,0,2,1:T(8,128)(2,1)} %copy-done.1) | copy-start | bytes 6291460
  173.7 11.5 %copy-start.5 = (bf16[3,32]{1,0:T(4,128)(2,1)S(1)}, bf16[3,32]{1,0:T(4,128)(2,1)}, u32[]{:S(2)}) copy-start(bf16[3,32]{1,0:T(4,128)(2,1)} %param.15) | copy-start | bytes 580
where the time goes:
time: 190 us; the launch traced here: 189 us
  matrix products  108 us (57%)
  local copies, waits for them, and re-layouts  36.2 us (19%)
  starting transfers between devices  25.1 us (13%)
  waiting for transfers between devices  11.6 us (6%)
  other arithmetic  7.97 us (4%)
    dot_general x26, matrix products, conv_volume(): jnp.einsum('oc,czxy->ozxy', weights[:, :, offset_z, offset_x, offset_y],...  46.6 us
    dot_general x9, matrix products, conv_plane(): jnp.einsum('oc,czxy->ozxy', weights[:, :, offset_x, offset_y], window, pr...  30.4 us
    dot_general x1, matrix products, per_device(): jnp.einsum('ocab,czxy->ozxayb', w_up, deep, preferred_element_type=jnp.fl...  20.8 us
    ppermute x4, starting transfers between devices, extended(): before = lax.ppermute(last, axis, up)  12.1 us
    reshape x1, local copies, waits for them, and re-layouts, per_device(): raised = raised.reshape(channels, depth_z, width_x, length_y)  11.5 us
    transpose x1, local copies, waits for them, and re-layouts, per_device(): jnp.einsum('ocab,czxy->ozxayb', w_up, deep, preferred_element_type=jnp.fl...  11 us
    ppermute x4, waiting for transfers between devices, extended(): after = lax.ppermute(leading, axis, down)  9.95 us
    ppermute x4, starting transfers between devices, extended(): after = lax.ppermute(leading, axis, down)  8.49 us
  transfers between devices with their start and end apart: 9, of which 5 were waited for; matrix products, arithmetic and copies ran while one was open for 5% of the time, Pallas kernels for 0%

commit v1 on v0

--- a/solution.py
+++ b/solution.py
@@ -67,7 +67,9 @@
 
 
 def per_device(raw, tissue, w_emb, w_one, w_down, w_deep, w_up, w_out):
-    sections = lax.all_to_all(raw, "blk", split_axis=1, concat_axis=0, tiled=True)
+    sections = jnp.concatenate(
+        lax.all_to_all(jnp.stack(jnp.split(raw, lax.axis_size("blk"), axis=1)), "blk", 0, 0), axis=0
+    )
     depth_z, width_x, length_y = sections.shape
     blocks_y = tissue.shape[2]
     span_y = length_y // blocks_y

time: 190 us -> 197 us (1.037)
  local copies, waits for them, and re-layouts: 36.2 us -> 44.4 us
    unnamed x19 -> x21, local copies, waits for them, and re-layouts: 2.22 us -> 9.1 us
where the time goes in v1:
time: 197 us; the launch traced here: 196 us
  matrix products  108 us (55%)
  local copies, waits for them, and re-layouts  44.4 us (23%)
  starting transfers between devices  25.1 us (13%)
  waiting for transfers between devices  11.6 us (6%)
  other arithmetic  6.96 us (4%)
    dot_general x26, matrix products, conv_volume(): jnp.einsum('oc,czxy->ozxy', weights[:, :, offset_z, offset_x, offset_y],...  46.7 us
    dot_general x9, matrix products, conv_plane(): jnp.einsum('oc,czxy->ozxy', weights[:, :, offset_x, offset_y], window, pr...  30.4 us
    dot_general x1, matrix products, per_device(): jnp.einsum('ocab,czxy->ozxayb', w_up, deep, preferred_element_type=jnp.fl...  20.8 us
    ppermute x4, starting transfers between devices, extended(): before = lax.ppermute(last, axis, up)  12.1 us
    reshape x1, local copies, waits for them, and re-layouts, per_device(): raised = raised.reshape(channels, depth_z, width_x, length_y)  11.6 us
    transpose x1, local copies, waits for them, and re-layouts, per_device(): jnp.einsum('ocab,czxy->ozxayb', w_up, deep, preferred_element_type=jnp.fl...  11 us
    ppermute x4, waiting for transfers between devices, extended(): after = lax.ppermute(leading, axis, down)  9.93 us
    unnamed x21, local copies, waits for them, and re-layouts  9.1 us
  transfers between devices with their start and end apart: 9, of which 5 were waited for; matrix products, arithmetic and copies ran while one was open for 5% of the time, Pallas kernels for 0%

profile of v1, /device:TPU:11, one launch (start us, length us, event | category | flops | bytes accessed | tf_op | source)
XLA Modules:
  0.0 196.2 jit_solution(9240552829451813618)
XLA Ops:
  10.4 4.6 %all-to-all-start = ((bf16[8,1,16,256]{3,2,1,0:T(8,128)(2,1)}), bf16[8,1,16,256]{3,2,1,0:T(8,128)(2,1)S(1)}, u32[]{:S(2)}, u32[]{:S(2)}) async-start(bf16[8,1,16,256]{3,2,1,0:T(8,128)(2,1)} %constant_dynamic-update-slice_fusion), calls=%async_computation | async-start | bytes 131072 | tf_op jit(solution)/shard_map/all_to_all | solution.py:71
  18.3 3.5 %collective-permute-start = (bf16[8,1,256]{2,1,0:T(2,128)(2,1)S(1)}, bf16[8,1,256]{2,1,0:T(2,128)(2,1)S(1)}, u32[]{:S(2)}, u32[]{:S(2)}) collective-permute-start(bf16[8,1,256]{2,1,0:T(2,128)(2,1)S(1)} %get-tuple-element.21), channel_id=1, source_target_pairs={{0,1},{1,2},{2,3},{3,4},{4,5},{5,6},{6,7},{8,9},{9,10},{10,11},{11... | collective-permute-start | bytes 12296 | tf_op jit(solution)/shard_map/ppermute | solution.py:14
  21.9 1.9 collective-permute-start.1
  24.0 3.8 %collective-permute-done.1 = bf16[8,1,256]{2,1,0:T(2,128)(2,1)S(1)} collective-permute-done((bf16[8,1,256]{2,1,0:T(2,128)(2,1)S(1)}, bf16[8,1,256]{2,1,0:T(2,128)(2,1)S(1)}, u32[]{:S(2)}, u32[]{:S(2)}) %collective-permute-start.1) | collective-permute-done | bytes 4128 | tf_op jit(solution)/shard_map/ppermute | solution.py:15
  31.7 1.9 collective-permute-start.2
  33.6 2.6 %collective-permute-start.3 = (bf16[32,8,1,256]{3,0,2,1:T(8,128)(2,1)S(1)}, bf16[32,8,1,256]{3,0,2,1:T(8,128)(2,1)S(1)}, u32[]{:S(2)}, u32[]{:S(2)}) collective-permute-start(bf16[32,8,1,256]{3,0,2,1:T(8,128)(2,1)S(1)} %get-tuple-element.6), channel_id=1, source_target_pairs={{1,0},{2,1},{3,2},{4,3},{5,4},{6,5},{7,6},{9,8},{10,9},{11,10},{12... | collective-permute-start | bytes 393224 | tf_op jit(solution)/shard_map/ppermute | solution.py:15
  36.2 2.6 %fusion.175 = f32[8,16,256,32]{2,3,1,0:T(8,128)} fusion(bf16[32,8,16,256]{3,0,2,1:T(8,128)(2,1)S(1)} %fusion.41, bf16[32,32,3,3]{1,0,3,2:T(8,128)(2,1)S(1)} %copy-done.4), kind=kOutput, calls=%fused_computation.214 | convolution fusion | flops 67108864 | bytes 6299648 | tf_op jit(solution)/shard_map/oc,czxy->ozxy/dot_general | solution.py:38
  38.9 2.0 %collective-permute-done.3 = bf16[32,8,1,256]{3,0,2,1:T(8,128)(2,1)S(1)} collective-permute-done((bf16[32,8,1,256]{3,0,2,1:T(8,128)(2,1)S(1)}, bf16[32,8,1,256]{3,0,2,1:T(8,128)(2,1)S(1)}, u32[]{:S(2)}, u32[]{:S(2)}) %collective-permute-start.3) | collective-permute-done | bytes 131104 | tf_op jit(solution)/shard_map/ppermute | solution.py:15
  40.8 2.4 %fusion.8 = bf16[32,8,18,258]{3,0,2,1:T(8,128)(2,1)S(1)} fusion(bf16[32,8,1,256]{3,0,2,1:T(8,128)(2,1)S(1)} %collective-permute-done.3, bf16[32,8,16,256]{3,0,2,1:T(8,128)(2,1)S(1)} %fusion.41, bf16[32,8,1,256]{3,0,2,1:T(8,128)(2,1)S(1)} %collective-permute-done.2), kind=kLoop, calls=%fused_computation.15 | loop fusion | flops 14266368 | bytes 4737024 | tf_op jit(solution)/shard_map/concatenate | solution.py:16
  43.2 2.7 %fusion.20 = f32[8,16,256,32]{2,3,1,0:T(8,128)} fusion(bf16[32,8,18,258]{3,0,2,1:T(8,128)(2,1)S(1)} %fusion.8, bf16[32,32,3,3]{1,0,3,2:T(8,128)(2,1)S(1)} %copy-done.4), kind=kOutput, calls=%fused_computation.29 | convolution fusion | flops 67108864 | bytes 6299648 | tf_op jit(solution)/shard_map/oc,czxy->ozxy/dot_general | solution.py:38
  45.9 2.8 %fusion.22 = f32[8,16,256,32]{2,3,1,0:T(8,128)} fusion(bf16[32,8,18,258]{3,0,2,1:T(8,128)(2,1)S(1)} %fusion.8, bf16[32,32,3,3]{1,0,3,2:T(8,128)(2,1)S(1)} %copy-done.4), kind=kOutput, calls=%fused_computation.31 | convolution fusion | flops 67108864 | bytes 6299648 | tf_op jit(solution)/shard_map/oc,czxy->ozxy/dot_general | solution.py:38
  48.7 2.6 %fusion.24 = f32[8,16,256,32]{2,3,1,0:T(8,128)} fusion(bf16[32,8,18,258]{3,0,2,1:T(8,128)(2,1)S(1)} %fusion.8, bf16[32,32,3,3]{1,0,3,2:T(8,128)(2,1)S(1)} %copy-done.4), kind=kOutput, calls=%fused_computation.33 | convolution fusion | flops 67108864 | bytes 6299648 | tf_op jit(solution)/shard_map/oc,czxy->ozxy/dot_general | solution.py:38
  51.3 2.8 %fusion.26 = f32[8,16,256,32]{2,3,1,0:T(8,128)} fusion(bf16[32,8,18,258]{3,0,2,1:T(8,128)(2,1)S(1)} %fusion.8, bf16[32,32,3,3]{1,0,3,2:T(8,128)(2,1)S(1)} %copy-done.4), kind=kOutput, calls=%fused_computation.35 | convolution fusion | flops 67108864 | bytes 6299648 | tf_op jit(solution)/shard_map/oc,czxy->ozxy/dot_general | solution.py:38
  54.1 2.7 %fusion.30 = f32[8,16,256,32]{2,3,1,0:T(8,128)} fusion(bf16[32,8,18,258]{3,0,2,1:T(8,128)(2,1)S(1)} %fusion.8, bf16[32,32,3,3]{1,0,3,2:T(8,128)(2,1)S(1)} %copy-done.4), kind=kOutput, calls=%fused_computation.40 | convolution fusion | flops 67108864 | bytes 6299648 | tf_op jit(solution)/shard_map/oc,czxy->ozxy/dot_general | solution.py:38
  57.5 2.6 %fusion.18 = f32[8,16,256,32]{2,3,1,0:T(8,128)} fusion(bf16[32,8,1,256]{3,0,2,1:T(8,128)(2,1)S(1)} %collective-permute-done.3, bf16[32,8,16,256]{3,0,2,1:T(8,128)(2,1)S(1)} %fusion.41, bf16[32,32,3,3]{1,0,3,2:T(8,128)(2,1)S(1)} %copy-done.4), kind=kOutput, calls=%fused_computation.27 | convolution fusion | flops 71303168 | bytes 6430720 | tf_op jit(solution)/shard_map/oc,czxy->ozxy/dot_general | solution.py:38
  60.1 10.9 %fusion.38 = bf16[32,8,16,256]{3,0,2,1:T(8,128)(2,1)S(1)} fusion(f32[256]{0:T(256)S(1)} %reshape.33, bf16[32,8,18,258]{3,0,2,1:T(8,128)(2,1)S(1)} %fusion.8, f32[8,16,256,32]{2,3,1,0:T(8,128)} %fusion.18, f32[8,16,256,32]{2,3,1,0:T(8,128)} %fusion.20, f32[8,16,256,32]{2,3,1,0:T(8,128)} %fusion.22, f32[8,16,256,32]{2,3,1,0:T(8,128)} %fusion.175, ...), kind=kOutput, calls=%fused_computation.59 | convolution fusion | flops 78643200 | bytes 37757952 | tf_op jit(solution)/shard_map/oc,czxy->ozxy/dot_general | solution.py:38
  71.0 6.7 %copy.167 = bf16[32,8,16,256]{0,1,3,2:T(8,128)(2,1)} copy(bf16[32,8,16,256]{3,0,2,1:T(8,128)(2,1)S(1)} %fusion.38) | data formatting | bytes 4194304 | tf_op jit(solution)/shard_map/convert_element_type | solution.py:90
  77.7 6.3 %fusion.45 = bf16[64,8,8,128]{3,0,2,1:T(8,128)(2,1)S(1)} fusion(bf16[32,8,8,2,128,2]{0,1,5,4,3,2:T(8,128)(2,1)} %bitcast.407, f32[128]{0:T(128)S(1)} %mul.67, bf16[64,32,2,2,1,1]{0,3,2,1,5,4:T(2,128)(2,1)S(1)} %bitcast.409), kind=kOutput, calls=%fused_computation.64 | convolution fusion | flops 135790592 | bytes 3162624 | tf_op jit(solution)/shard_map/ocab,czxayb->ozxy/dot_general | solution.py:92
  84.0 3.2 %collective-permute-start.4 = (bf16[64,1,8,128]{3,0,2,1:T(8,128)(2,1)S(1)}, bf16[64,1,8,128]{3,0,2,1:T(8,128)(2,1)S(1)}, u32[]{:S(2)}, u32[]{:S(2)}) collective-permute-start(bf16[64,1,8,128]{3,0,2,1:T(8,128)(2,1)S(1)} %get-tuple-element.11), channel_id=1, source_target_pairs={{0,8},{8,16},{16,24},{1,9},{9,17},{17,25},{2,10},{10,18},{18,26},{... | collective-permute-start | bytes 393224 | tf_op jit(solution)/shard_map/ppermute | solution.py:14
  87.2 2.1 %collective-permute-start.5 = (bf16[64,1,8,128]{3,0,2,1:T(8,128)(2,1)S(1)}, bf16[64,1,8,128]{3,0,2,1:T(8,128)(2,1)S(1)}, u32[]{:S(2)}, u32[]{:S(2)}) collective-permute-start(bf16[64,1,8,128]{3,0,2,1:T(8,128)(2,1)S(1)} %get-tuple-element.12), channel_id=1, source_target_pairs={{8,0},{16,8},{24,16},{9,1},{17,9},{25,17},{10,2},{18,10},{26,18},{... | collective-permute-start | bytes 393224 | tf_op jit(solution)/shard_map/ppermute | solution.py:15
  91.0 2.1 %collective-permute-done.5 = bf16[64,1,8,128]{3,0,2,1:T(8,128)(2,1)S(1)} collective-permute-done((bf16[64,1,8,128]{3,0,2,1:T(8,128)(2,1)S(1)}, bf16[64,1,8,128]{3,0,2,1:T(8,128)(2,1)S(1)}, u32[]{:S(2)}, u32[]{:S(2)}) %collective-permute-start.5) | collective-permute-done | bytes 131104 | tf_op jit(solution)/shard_map/ppermute | solution.py:15
  93.2 3.4 %collective-permute-start.6 = (bf16[64,10,1,128]{3,0,2,1:T(8,128)(2,1)S(1)}, bf16[64,10,1,128]{3,0,2,1:T(8,128)(2,1)S(1)}, u32[]{:S(2)}, u32[]{:S(2)}) collective-permute-start(bf16[64,10,1,128]{3,0,2,1:T(8,128)(2,1)S(1)} %get-tuple-element.9), channel_id=1, source_target_pairs={{0,1},{1,2},{2,3},{3,4},{4,5},{5,6},{6,7},{8,9},{9,10},{10,11},{11... | collective-permute-start | bytes 491528 | tf_op jit(solution)/shard_map/ppermute | solution.py:14
  96.5 1.9 collective-permute-start.7
  102.0 2.1 %collective-permute-done.7 = bf16[64,10,1,128]{3,0,2,1:T(8,128)(2,1)S(1)} collective-permute-done((bf16[64,10,1,128]{3,0,2,1:T(8,128)(2,1)S(1)}, bf16[64,10,1,128]{3,0,2,1:T(8,128)(2,1)S(1)}, u32[]{:S(2)}, u32[]{:S(2)}) %collective-permute-start.7) | collective-permute-done | bytes 163872 | tf_op jit(solution)/shard_map/ppermute | solution.py:15
  104.1 3.1 %select_maximum_fusion = bf16[64,10,10,130]{3,0,2,1:T(8,128)(2,1)S(1)} fusion(bf16[64,10,1,128]{3,0,2,1:T(8,128)(2,1)S(1)} %collective-permute-done.7, bf16[64,10,1,128]{3,0,2,1:T(8,128)(2,1)S(1)} %collective-permute-done.6, bf16[64,1,8,128]{3,0,2,1:T(8,128)(2,1)S(1)} %collective-permute-done.5, bf16[64,8,8,128]{3,0,2,1:T(8,128)(2,1)S(1)} %fusion.45, ...), kind=kLoop, calls=%fused_computation.16 | loop fusion | flops 14976000 | bytes 3302400 | tf_op jit(solution)/shard_map/concatenate | solution.py:16
  116.2 1.9 fusion.68
  123.4 1.9 fusion.78
  127.1 1.9 fusion.84
  149.1 20.8 %convolution_bitcast_fusion = f32[32,8,8,2,128,2]{4,0,5,3,2,1:T(8,128)} fusion(f32[8,8,128,64]{2,3,1,0:T(8,128)} %fusion.52, f32[8,8,128,64]{2,3,1,0:T(8,128)} %fusion.54, f32[8,8,128,64]{2,3,1,0:T(8,128)} %fusion.56, f32[8,8,128,64]{2,3,1,0:T(8,128)} %fusion.58, f32[8,8,128,64]{2,3,1,0:T(8,128)} %fusion.60, f32[8,8,128,64]{2,3,1,0:T(8,128)} %fusion.62, ...), kind=kOutput, calls=%fused_computation.23 | convolution fusion | flops 216530944 | bytes 59818496 | tf_op jit(solution)/shard_map/ocab,czxy->ozxayb/dot_general | solution.py:98
  169.9 11.0 %copy.171 = f32[32,8,8,2,128,2]{0,1,5,4,3,2:T(8,128)} copy(f32[32,8,8,2,128,2]{4,0,5,3,2,1:T(8,128)} %convolution_bitcast_fusion) | data formatting | bytes 8388608 | tf_op jit(solution)/shard_map/ocab,czxy->ozxayb/transpose | solution.py:98
  180.9 11.6 %copy.172 = f32[32,8,16,256]{3,0,2,1:T(8,128)} copy(f32[32,8,16,256]{0,1,3,2:T(8,128)} %bitcast.406) | data formatting | bytes 8388608 | tf_op jit(solution)/shard_map/reshape | solution.py:99
  192.5 2.9 %fusion.49 = f32[3,8,16,256]{3,0,2,1:T(4,128)S(1)} fusion(f32[32,8,16,256]{3,0,2,1:T(8,128)} %copy.172, bf16[32,8,16,256]{3,0,2,1:T(8,128)(2,1)S(1)} %copy-done.2, f32[256]{0:T(256)S(1)} %reshape.33, bf16[3,32]{1,0:T(4,128)(2,1)S(1)} %copy-done.5), kind=kOutput, calls=%fused_computation.66 | convolution fusion | flops 11632640 | bytes 6685888 | tf_op jit(solution)/shard_map/oc,czxy->ozxy/dot_general | solution.py:103
  (79 shorter events, 60.7 us)
Async XLA Ops:
  0.0 149.1 %copy-start = (bf16[32,64,2,2]{1,3,2,0:T(2,128)(2,1)S(1)}, bf16[32,64,2,2]{1,3,2,0:T(2,128)(2,1)}, u32[]{:S(2)}) copy-start(bf16[32,64,2,2]{1,3,2,0:T(2,128)(2,1)} %param.14) | copy-start | bytes 49156
  10.4 7.9 %all-to-all-start = ((bf16[8,1,16,256]{3,2,1,0:T(8,128)(2,1)}), bf16[8,1,16,256]{3,2,1,0:T(8,128)(2,1)S(1)}, u32[]{:S(2)}, u32[]{:S(2)}) async-start(bf16[8,1,16,256]{3,2,1,0:T(8,128)(2,1)} %constant_dynamic-update-slice_fusion), calls=%async_computation | async-start | bytes 131072 | tf_op jit(solution)/shard_map/all_to_all | solution.py:71
  18.3 5.6 %collective-permute-start = (bf16[8,1,256]{2,1,0:T(2,128)(2,1)S(1)}, bf16[8,1,256]{2,1,0:T(2,128)(2,1)S(1)}, u32[]{:S(2)}, u32[]{:S(2)}) collective-permute-start(bf16[8,1,256]{2,1,0:T(2,128)(2,1)S(1)} %get-tuple-element.21), channel_id=1, source_target_pairs={{0,1},{1,2},{2,3},{3,4},{4,5},{5,6},{6,7},{8,9},{9,10},{10,11},{11... | collective-permute-start | bytes 12296 | tf_op jit(solution)/shard_map/ppermute | solution.py:14
  21.9 5.9 %collective-permute-start.1 = (bf16[8,1,256]{2,1,0:T(2,128)(2,1)S(1)}, bf16[8,1,256]{2,1,0:T(2,128)(2,1)S(1)}, u32[]{:S(2)}, u32[]{:S(2)}) collective-permute-start(bf16[8,1,256]{2,1,0:T(2,128)(2,1)S(1)} %get-tuple-element.22), channel_id=1, source_target_pairs={{1,0},{2,1},{3,2},{4,3},{5,4},{6,5},{7,6},{9,8},{10,9},{11,10},{12... | collective-permute-start | bytes 12296 | tf_op jit(solution)/shard_map/ppermute | solution.py:15
  30.9 5.3 %copy-start.4 = (bf16[32,32,3,3]{1,0,3,2:T(8,128)(2,1)S(1)}, bf16[32,32,3,3]{1,0,3,2:T(8,128)(2,1)}, u32[]{:S(2)}) copy-start(bf16[32,32,3,3]{1,0,3,2:T(8,128)(2,1)} %param.11) | copy-start | bytes 55300
  31.7 7.2 %collective-permute-start.2 = (bf16[32,8,1,256]{3,0,2,1:T(8,128)(2,1)S(1)}, bf16[32,8,1,256]{3,0,2,1:T(8,128)(2,1)S(1)}, u32[]{:S(2)}, u32[]{:S(2)}) collective-permute-start(bf16[32,8,1,256]{3,0,2,1:T(8,128)(2,1)S(1)} %get-tuple-element.5), channel_id=1, source_target_pairs={{0,1},{1,2},{2,3},{3,4},{4,5},{5,6},{6,7},{8,9},{9,10},{10,11},{11... | collective-permute-start | bytes 393224 | tf_op jit(solution)/shard_map/ppermute | solution.py:14
  33.6 7.2 %collective-permute-start.3 = (bf16[32,8,1,256]{3,0,2,1:T(8,128)(2,1)S(1)}, bf16[32,8,1,256]{3,0,2,1:T(8,128)(2,1)S(1)}, u32[]{:S(2)}, u32[]{:S(2)}) collective-permute-start(bf16[32,8,1,256]{3,0,2,1:T(8,128)(2,1)S(1)} %get-tuple-element.6), channel_id=1, source_target_pairs={{1,0},{2,1},{3,2},{4,3},{5,4},{6,5},{7,6},{9,8},{10,9},{11,10},{12... | collective-permute-start | bytes 393224 | tf_op jit(solution)/shard_map/ppermute | solution.py:15
  71.0 6.7 %copy-start.1 = (bf16[32,8,16,256]{3,0,2,1:T(8,128)(2,1)}, bf16[32,8,16,256]{3,0,2,1:T(8,128)(2,1)S(1)}, u32[]{:S(2)}) copy-start(bf16[32,8,16,256]{3,0,2,1:T(8,128)(2,1)S(1)} %fusion.38) | copy-start | bytes 6291460
  71.0 6.7 %copy-start.6 = (bf16[64,32,2,2]{0,3,2,1:T(2,128)(2,1)S(1)}, bf16[64,32,2,2]{0,3,2,1:T(2,128)(2,1)}, u32[]{:S(2)}) copy-start(bf16[64,32,2,2]{0,3,2,1:T(2,128)(2,1)} %param.12) | copy-start | bytes 49156
  77.7 11.6 %copy-start.3 = (bf16[64,64,3,3,3]{1,0,4,3,2:T(8,128)(2,1)S(1)}, bf16[64,64,3,3,3]{1,0,4,3,2:T(8,128)(2,1)}, u32[]{:S(2)}) copy-start(bf16[64,64,3,3,3]{1,0,4,3,2:T(8,128)(2,1)} %param.13) | copy-start | bytes 663556
  84.0 7.0 %collective-permute-start.4 = (bf16[64,1,8,128]{3,0,2,1:T(8,128)(2,1)S(1)}, bf16[64,1,8,128]{3,0,2,1:T(8,128)(2,1)S(1)}, u32[]{:S(2)}, u32[]{:S(2)}) collective-permute-start(bf16[64,1,8,128]{3,0,2,1:T(8,128)(2,1)S(1)} %get-tuple-element.11), channel_id=1, source_target_pairs={{0,8},{8,16},{16,24},{1,9},{9,17},{17,25},{2,10},{10,18},{18,26},{... | collective-permute-start | bytes 393224 | tf_op jit(solution)/shard_map/ppermute | solution.py:14
  87.2 5.9 %collective-permute-start.5 = (bf16[64,1,8,128]{3,0,2,1:T(8,128)(2,1)S(1)}, bf16[64,1,8,128]{3,0,2,1:T(8,128)(2,1)S(1)}, u32[]{:S(2)}, u32[]{:S(2)}) collective-permute-start(bf16[64,1,8,128]{3,0,2,1:T(8,128)(2,1)S(1)} %get-tuple-element.12), channel_id=1, source_target_pairs={{8,0},{16,8},{24,16},{9,1},{17,9},{25,17},{10,2},{18,10},{26,18},{... | collective-permute-start | bytes 393224 | tf_op jit(solution)/shard_map/ppermute | solution.py:15
  93.2 8.8 %collective-permute-start.6 = (bf16[64,10,1,128]{3,0,2,1:T(8,128)(2,1)S(1)}, bf16[64,10,1,128]{3,0,2,1:T(8,128)(2,1)S(1)}, u32[]{:S(2)}, u32[]{:S(2)}) collective-permute-start(bf16[64,10,1,128]{3,0,2,1:T(8,128)(2,1)S(1)} %get-tuple-element.9), channel_id=1, source_target_pairs={{0,1},{1,2},{2,3},{3,4},{4,5},{5,6},{6,7},{8,9},{9,10},{10,11},{11... | collective-permute-start | bytes 491528 | tf_op jit(solution)/shard_map/ppermute | solution.py:14
  96.5 7.5 %collective-permute-start.7 = (bf16[64,10,1,128]{3,0,2,1:T(8,128)(2,1)S(1)}, bf16[64,10,1,128]{3,0,2,1:T(8,128)(2,1)S(1)}, u32[]{:S(2)}, u32[]{:S(2)}) collective-permute-start(bf16[64,10,1,128]{3,0,2,1:T(8,128)(2,1)S(1)} %get-tuple-element.10), channel_id=1, source_target_pairs={{1,0},{2,1},{3,2},{4,3},{5,4},{6,5},{7,6},{9,8},{10,9},{11,10},{12... | collective-permute-start | bytes 491528 | tf_op jit(solution)/shard_map/ppermute | solution.py:15
  180.9 11.6 %copy-start.2 = (bf16[32,8,16,256]{3,0,2,1:T(8,128)(2,1)S(1)}, bf16[32,8,16,256]{3,0,2,1:T(8,128)(2,1)}, u32[]{:S(2)}) copy-start(bf16[32,8,16,256]{3,0,2,1:T(8,128)(2,1)} %copy-done.1) | copy-start | bytes 6291460
  180.9 11.6 %copy-start.5 = (bf16[3,32]{1,0:T(4,128)(2,1)S(1)}, bf16[3,32]{1,0:T(4,128)(2,1)}, u32[]{:S(2)}) copy-start(bf16[3,32]{1,0:T(4,128)(2,1)} %param.15) | copy-start | bytes 580
